TPU v7x, 128 devices: a whole 4x4x4 slice. The times are simulated.
128 devices in a mesh: blk: 32 (over z_hi, y, x), head: 4 (over z_lo, core).
Axes of the slice: x: 4, y: 4, z: 4 (z_hi: 2, z_lo: 2; z = z_hi * 2 + z_lo), core: 2. Of those that a mesh axis runs over, the one named last changes fastest.
Arguments:
- tokens: bfloat16 [12288, 1024], P(('blk', 'head')), may hold values from -18 to 18
- block_order: int32 [64], replicated, may hold values from 0 to 63, as said below
- request_lengths: int32 [9], replicated, may hold values from 1 to 9216, 12288 in all
- enc_lengths: int32 [9], replicated, may hold values from 1 to 512, 2048 in all
- w_qkv: bfloat16 [3, 1024, 1024], P(None, None, 'head'), may hold values from -0.1875 to 0.1875
- w_out: bfloat16 [1024, 1024], P('head'), may hold values from -0.1875 to 0.1875
- enc_kv: bfloat16 [2, 2048, 1024], P(None, 'blk', 'head'), may hold values from -18 to 18
- w_cq: bfloat16 [1024, 1024], replicated, may hold values from -0.1875 to 0.1875
- w_co: bfloat16 [1024, 1024], replicated, may hold values from -0.1875 to 0.1875
- w_up: bfloat16 [1024, 4096], replicated, may hold values from -0.1875 to 0.1875
- w_down: bfloat16 [4096, 1024], replicated, may hold values from -0.09375 to 0.09375
- w_next: bfloat16 [3, 1024, 1024], P(None, None, 'head'), may hold values from -0.1875 to 0.1875
Outputs:
- output: float32 [12288, 1024], P(('blk', 'head'))
- cache: bfloat16 [2, 12288, 1024], P(None, 'blk', 'head')
- next_qkv: float32 [3, 12288, 1024], P(None, 'blk', 'head')
Inputs may be any that keep to these rules, and one draw needn't show every extreme that they name: `block_order`: each half-block index appears once, and stored half-blocks 2i and 2i + 1 hold position blocks that add up to 63. `request_lengths`: the lengths sum to 12288. `enc_lengths`: the lengths sum to 2048.
All inputs are finite; a program needn't handle non-finite values.
Results may differ from a plain program's by a relative error of at most 0.024.
Values may be sent and summed in bfloat16 or wider, within the bound.
A program may use at most 128 MiB of HBM per device.

v0:
```python
import math

import jax
import jax.numpy as jnp
from jax import lax
from jax.sharding import PartitionSpec as P

HEADS = 16


NEGATIVE = -1e30
SCALING = 0.125
EPSILON = 1e-05


def normalize(matrix):
    center = matrix - jnp.mean(matrix, axis=-1, keepdims=True)
    return center * lax.rsqrt(jnp.mean(center * center, axis=-1, keepdims=True) + EPSILON)


def position_of(order_table, indices, halfway):
    slots = jnp.arange(order_table.shape[0], dtype=jnp.int32)
    picked = jnp.sum(
        jnp.where((indices // halfway)[:, None] == slots[None, :], order_table[None, :], 0), axis=1
    )
    return picked * halfway + indices % halfway


def group_of(places, lengths):
    ends = jnp.cumsum(lengths)
    return jnp.sum((places[:, None] >= ends[None, :]).astype(jnp.int32), axis=1)


def online_update(carried, queries, key_rows, value_rows, visible):
    maxima, totals, running = carried
    heads_here = queries.shape[1]
    key_split = key_rows.reshape(key_rows.shape[0], heads_here, -1)
    value_split = value_rows.reshape(value_rows.shape[0], heads_here, -1)
    scores = (
        jnp.einsum("qhd,khd->qhk", queries, key_split, preferred_element_type=jnp.float32) * SCALING
    )
    scores = jnp.where(visible[:, None, :], scores, NEGATIVE)
    updated = jnp.maximum(maxima, jnp.max(scores, axis=2))
    factor = jnp.exp(maxima - updated)
    weights = jnp.exp(scores - updated[:, :, None])
    totals = totals * factor + jnp.sum(weights, axis=2)
    running = running * factor[:, :, None] + jnp.einsum(
        "qhk,khd->qhd",
        weights.astype(jnp.bfloat16),
        value_split,
        preferred_element_type=jnp.float32,
    )
    return (updated, totals, running)


def sweep(
    carried, queries, key_rows, value_rows, key_places, key_groups, query_places, query_groups
):
    length = key_rows.shape[0]
    block_size = math.gcd(length, 2048)
    blocks_count = length // block_size
    key_blocks = key_rows.reshape(blocks_count, block_size, key_rows.shape[1])
    value_blocks = value_rows.reshape(blocks_count, block_size, value_rows.shape[1])
    group_blocks = key_groups.reshape(blocks_count, block_size)
    if key_places is None:
        place_blocks = group_blocks
    else:
        place_blocks = key_places.reshape(blocks_count, block_size)

    def advance(status, element):
        key_block, value_block, place_block, group_block = element
        visible = group_block[None, :] == query_groups[:, None]
        if key_places is None:
            return (online_update(status, queries, key_block, value_block, visible), None)
        visible = visible & (place_block[None, :] <= query_places[:, None])
        updated = online_update(status, queries, key_block, value_block, visible)
        return (updated, None)

    carried, unused = lax.scan(
        advance, carried, (key_blocks, value_blocks, place_blocks, group_blocks)
    )
    return carried


def empty_state(count_q, heads_here, head_width):
    return (
        jnp.full((count_q, heads_here), NEGATIVE, jnp.float32),
        jnp.zeros((count_q, heads_here), jnp.float32),
        jnp.zeros((count_q, heads_here, head_width), jnp.float32),
    )


def finish(carried):
    maxima, totals, running = carried
    return (running / totals[:, :, None]).reshape(running.shape[0], -1).astype(jnp.bfloat16)


def on_device(
    tokens,
    block_order,
    request_lengths,
    enc_lengths,
    w_qkv,
    w_out,
    enc_kv,
    w_cq,
    w_co,
    w_up,
    w_down,
    w_next,
):
    rows_here = tokens.shape[0]
    model_width = tokens.shape[1]
    group_size = lax.axis_size("head")
    cycle_size = lax.axis_size("blk")
    block_rows = rows_here * group_size
    halfway = block_rows // 2
    group_width = w_qkv.shape[2]
    head_width = model_width // HEADS
    group_heads = group_width // head_width
    gathered = lax.all_gather(tokens, "head", axis=0, tiled=True)
    projected = jnp.einsum(
        "td,cde->cte", gathered, w_qkv, preferred_element_type=jnp.float32
    ).astype(jnp.bfloat16)
    cycle_index = lax.axis_index("blk")
    block_start = cycle_index * block_rows
    query_places = position_of(
        block_order, block_start + jnp.arange(block_rows, dtype=jnp.int32), halfway
    )
    query_groups = group_of(query_places, request_lengths)
    queries = projected[0].reshape(block_rows, group_heads, head_width)
    start_state = empty_state(block_rows, group_heads, head_width)
    slots = jnp.arange(2 * cycle_size, dtype=jnp.int32)
    holders = jnp.sum(jnp.where(block_order[:, None] == slots[None, :], slots[:, None], 0), axis=0)
    start_carry = (start_state, jnp.zeros((1,), jnp.bfloat16))
    shards = (
        lax.all_gather(projected[1], "blk", axis=0, tiled=True),
        lax.all_gather(projected[2], "blk", axis=0, tiled=True),
    )
    shard_length = shards[0].shape[0]
    key_places = position_of(block_order, jnp.arange(shard_length, dtype=jnp.int32), halfway)
    key_groups = group_of(key_places, request_lengths)
    final_state = sweep(
        start_carry[0],
        queries,
        shards[0],
        shards[1],
        key_places,
        key_groups,
        query_places,
        query_groups,
    )
    attended = finish(final_state)
    pair = lax.dynamic_slice_in_dim(block_order, 2 * cycle_index, 2, 0)
    targets = pair // 2
    halves = projected[1:].reshape(2, 2, halfway, group_width)
    cycle_slots = jnp.arange(cycle_size, dtype=jnp.int32)
    outgoing = jnp.where(
        (cycle_slots == targets[0])[None, :, None, None],
        halves[:, 0][:, None],
        jnp.where(
            (cycle_slots == targets[1])[None, :, None, None],
            halves[:, 1][:, None],
            jnp.zeros((), jnp.bfloat16),
        ),
    )
    incoming = lax.all_to_all(outgoing, "blk", split_axis=1, concat_axis=1, tiled=True)
    first_source = lax.dynamic_index_in_dim(holders, 2 * cycle_index, 0, keepdims=False) // 2
    second_source = lax.dynamic_index_in_dim(holders, 2 * cycle_index + 1, 0, keepdims=False) // 2
    cache = jnp.concatenate(
        [
            lax.dynamic_index_in_dim(incoming, first_source, 1, keepdims=False),
            lax.dynamic_index_in_dim(incoming, second_source, 1, keepdims=False),
        ],
        axis=1,
    )
    mixed = lax.psum_scatter(
        jnp.dot(attended, w_out, preferred_element_type=jnp.float32),
        "head",
        scatter_dimension=0,
        tiled=True,
    )
    hidden = normalize(mixed + tokens.astype(jnp.float32))
    hidden_b = hidden.astype(jnp.bfloat16)
    member = lax.axis_index("head")
    own_places = lax.dynamic_slice_in_dim(query_places, member * rows_here, rows_here, 0)
    own_groups = group_of(own_places, request_lengths)
    cross_query = jnp.dot(hidden_b, w_cq, preferred_element_type=jnp.float32).astype(jnp.bfloat16)
    cross_split = cross_query.reshape(rows_here, HEADS, head_width)
    widened = lax.all_gather(enc_kv, "head", axis=2, tiled=True)
    shards = lax.all_gather(widened, "blk", axis=1, tiled=True)
    shard_length = shards.shape[1]
    encoder_groups = group_of(jnp.arange(shard_length, dtype=jnp.int32), enc_lengths)
    crossed = finish(
        sweep(
            empty_state(rows_here, HEADS, head_width),
            cross_split,
            shards[0],
            shards[1],
            None,
            encoder_groups,
            None,
            own_groups,
        )
    )
    summed = jnp.dot(crossed, w_co, preferred_element_type=jnp.float32)
    second = normalize(summed + hidden)
    second_b = second.astype(jnp.bfloat16)
    inner = jax.nn.gelu(
        jnp.dot(second_b, w_up, preferred_element_type=jnp.float32), approximate=False
    ).astype(jnp.bfloat16)
    output = normalize(jnp.dot(inner, w_down, preferred_element_type=jnp.float32) + second)
    output_b = output.astype(jnp.bfloat16)
    block_output = lax.all_gather(output_b, "head", axis=0, tiled=True)
    next_qkv = jnp.einsum("td,cde->cte", block_output, w_next, preferred_element_type=jnp.float32)
    return (output, cache, next_qkv)


def solution(mesh):
    in_specs = (
        P(("blk", "head"), None),
        P(),
        P(),
        P(),
        P(None, None, "head"),
        P("head", None),
        P(None, "blk", "head"),
        P(),
        P(),
        P(),
        P(),
        P(None, None, "head"),
    )
    out_specs = (P(("blk", "head"), None), P(None, "blk", "head"), P(None, "blk", "head"))
    return jax.shard_map(
        on_device, mesh=mesh, in_specs=in_specs, out_specs=out_specs, check_vma=False
    )
```

profile of v0, /device:TPU:1, one launch (start us, length us, event | category | flops | bytes accessed | tf_op | source)
XLA Modules:
  0.0 678.4 jit_solution(2549490070128636175)
XLA Ops:
  7.2 10.7 %all_gather.18 = bf16[384,1024]{1,0:T(8,128)(2,1)S(1)} all-gather(bf16[96,1024]{1,0:T(8,128)(2,1)} %param.14), channel_id=1, replica_groups=mesh['blk'=32,'head'=4] {'head'}, dimensions={0}, use_global_device_ids=true | all-gather | bytes 983040 | tf_op jit(solution)/shard_map/all_gather | solution.py:121
  25.4 97.8 %all-gather.8.cloned.1.call-done = bf16[1,12288,256]{1,2,0:T(8,128)(2,1)} async-done(((bf16[1,384,256]{1,2,0:T(8,128)(2,1)}), bf16[1,12288,256]{1,2,0:T(8,128)(2,1)}) %all-gather.8.cloned.1.call-update) | async-done | bytes 6291472 | tf_op jit(solution)/shard_map/all_gather | solution.py:137
  123.3 8.7 %copy.36 = bf16[1,12288,256]{2,1,0:T(8,128)(2,1)} copy(bf16[1,12288,256]{1,2,0:T(8,128)(2,1)} %all-gather.8.cloned.1.call-done) | data formatting | bytes 12582912 | tf_op jit(solution)/shard_map/all_gather | solution.py:137
  132.0 92.0 %all-gather.10.cloned.1.call-done = bf16[1,12288,256]{1,2,0:T(8,128)(2,1)} async-done(((bf16[1,384,256]{1,2,0:T(8,128)(2,1)}), bf16[1,12288,256]{1,2,0:T(8,128)(2,1)}) %all-gather.10.cloned.1.call-update) | async-done | bytes 6291472 | tf_op jit(solution)/shard_map/all_gather | solution.py:138
  224.0 8.6 %copy.37 = bf16[1,12288,256]{2,1,0:T(8,128)(2,1)} copy(bf16[1,12288,256]{1,2,0:T(8,128)(2,1)} %all-gather.10.cloned.1.call-done) | data formatting | bytes 12582912 | tf_op jit(solution)/shard_map/all_gather | solution.py:138
  232.6 196.6 %while.3 = (s32[]{:T(128)}, f32[384,4]{0,1:T(4,128)S(1)}, f32[384,4]{0,1:T(4,128)S(1)}, f32[384,4,64]{0,2,1:T(8,128)S(1)}, s32[6,2048]{1,0:T(8,128)}, /*index=5*...) while((s32[]{:T(128)}, f32[384,4]{0,1:T(4,128)S(1)}, ...), condition=%wide.region_11.12_spmd.clone, body=%wide.region_8.11_spmd.clone.sunk | while | flops 842571264 | bytes 52513932 | solution.py:79
  240.3 8.1 %fusion.171 = (f32[384,4]{0,1:T(4,128)S(1)}, f32[4,2048,384]{2,1,0:T(8,128)}) fusion(pred[384,2048]{0,1:T(8,128)(4,1)S(1)} %compare_and_fusion.2, bf16[2048,4,64]{0,2,1:T(8,128)(2,1)} %bitcast.119, bf16[384,4,64]{0,2,1:T(8,128)(2,1)S(1)} %get-tuple-element.334), kind=kOutput, calls=%fused_computation.4.clone.1 | convolution fusion | flops 412088832 | bytes 14620672 | tf_op jit(solution)/shard_map/while/body/eval_jaxpr/qhd,khd->qhk/dot_general | solution.py:40
  257.1 8.3 %fusion.174 = f32[384,4,64]{0,2,1:T(8,128)S(1)} fusion(bf16[2048,4,64]{0,2,1:T(8,128)(2,1)} %bitcast.120, f32[4,2048,384]{2,1,0:T(8,128)} %get-tuple-element.295, f32[384,4]{0,1:T(4,128)S(1)} %select_maximum_fusion.2, pred[384,2048]{0,1:T(8,128)(4,1)S(1)} %compare_and_fusion.2, f32[384,4,64]{0,2,1:T(8,128)S(1)} %get-tuple-element.315, ...), kind=kOutput, calls=%fused_computation.9.clone.1 | convolution fusion | flops 415531008 | bytes 15216641 | tf_op jit(solution)/shard_map/while/body/eval_jaxpr/qhk,khd->qhd/dot_general | solution.py:47
  273.1 8.1 %fusion.171 = (f32[384,4]{0,1:T(4,128)S(1)}, f32[4,2048,384]{2,1,0:T(8,128)}) fusion(pred[384,2048]{0,1:T(8,128)(4,1)S(1)} %compare_and_fusion.2, bf16[2048,4,64]{0,2,1:T(8,128)(2,1)} %bitcast.119, bf16[384,4,64]{0,2,1:T(8,128)(2,1)S(1)} %get-tuple-element.334), kind=kOutput, calls=%fused_computation.4.clone.1 | convolution fusion | flops 412088832 | bytes 14620672 | tf_op jit(solution)/shard_map/while/body/eval_jaxpr/qhd,khd->qhk/dot_general | solution.py:40
  289.8 8.3 %fusion.174 = f32[384,4,64]{0,2,1:T(8,128)S(1)} fusion(bf16[2048,4,64]{0,2,1:T(8,128)(2,1)} %bitcast.120, f32[4,2048,384]{2,1,0:T(8,128)} %get-tuple-element.295, f32[384,4]{0,1:T(4,128)S(1)} %select_maximum_fusion.2, pred[384,2048]{0,1:T(8,128)(4,1)S(1)} %compare_and_fusion.2, f32[384,4,64]{0,2,1:T(8,128)S(1)} %get-tuple-element.315, ...), kind=kOutput, calls=%fused_computation.9.clone.1 | convolution fusion | flops 415531008 | bytes 15216641 | tf_op jit(solution)/shard_map/while/body/eval_jaxpr/qhk,khd->qhd/dot_general | solution.py:47
  305.9 8.1 %fusion.171 = (f32[384,4]{0,1:T(4,128)S(1)}, f32[4,2048,384]{2,1,0:T(8,128)}) fusion(pred[384,2048]{0,1:T(8,128)(4,1)S(1)} %compare_and_fusion.2, bf16[2048,4,64]{0,2,1:T(8,128)(2,1)} %bitcast.119, bf16[384,4,64]{0,2,1:T(8,128)(2,1)S(1)} %get-tuple-element.334), kind=kOutput, calls=%fused_computation.4.clone.1 | convolution fusion | flops 412088832 | bytes 14620672 | tf_op jit(solution)/shard_map/while/body/eval_jaxpr/qhd,khd->qhk/dot_general | solution.py:40
  322.6 8.3 %fusion.174 = f32[384,4,64]{0,2,1:T(8,128)S(1)} fusion(bf16[2048,4,64]{0,2,1:T(8,128)(2,1)} %bitcast.120, f32[4,2048,384]{2,1,0:T(8,128)} %get-tuple-element.295, f32[384,4]{0,1:T(4,128)S(1)} %select_maximum_fusion.2, pred[384,2048]{0,1:T(8,128)(4,1)S(1)} %compare_and_fusion.2, f32[384,4,64]{0,2,1:T(8,128)S(1)} %get-tuple-element.315, ...), kind=kOutput, calls=%fused_computation.9.clone.1 | convolution fusion | flops 415531008 | bytes 15216641 | tf_op jit(solution)/shard_map/while/body/eval_jaxpr/qhk,khd->qhd/dot_general | solution.py:47
  338.6 8.1 %fusion.171 = (f32[384,4]{0,1:T(4,128)S(1)}, f32[4,2048,384]{2,1,0:T(8,128)}) fusion(pred[384,2048]{0,1:T(8,128)(4,1)S(1)} %compare_and_fusion.2, bf16[2048,4,64]{0,2,1:T(8,128)(2,1)} %bitcast.119, bf16[384,4,64]{0,2,1:T(8,128)(2,1)S(1)} %get-tuple-element.334), kind=kOutput, calls=%fused_computation.4.clone.1 | convolution fusion | flops 412088832 | bytes 14620672 | tf_op jit(solution)/shard_map/while/body/eval_jaxpr/qhd,khd->qhk/dot_general | solution.py:40
  355.4 8.3 %fusion.174 = f32[384,4,64]{0,2,1:T(8,128)S(1)} fusion(bf16[2048,4,64]{0,2,1:T(8,128)(2,1)} %bitcast.120, f32[4,2048,384]{2,1,0:T(8,128)} %get-tuple-element.295, f32[384,4]{0,1:T(4,128)S(1)} %select_maximum_fusion.2, pred[384,2048]{0,1:T(8,128)(4,1)S(1)} %compare_and_fusion.2, f32[384,4,64]{0,2,1:T(8,128)S(1)} %get-tuple-element.315, ...), kind=kOutput, calls=%fused_computation.9.clone.1 | convolution fusion | flops 415531008 | bytes 15216641 | tf_op jit(solution)/shard_map/while/body/eval_jaxpr/qhk,khd->qhd/dot_general | solution.py:47
  371.4 8.1 %fusion.171 = (f32[384,4]{0,1:T(4,128)S(1)}, f32[4,2048,384]{2,1,0:T(8,128)}) fusion(pred[384,2048]{0,1:T(8,128)(4,1)S(1)} %compare_and_fusion.2, bf16[2048,4,64]{0,2,1:T(8,128)(2,1)} %bitcast.119, bf16[384,4,64]{0,2,1:T(8,128)(2,1)S(1)} %get-tuple-element.334), kind=kOutput, calls=%fused_computation.4.clone.1 | convolution fusion | flops 412088832 | bytes 14620672 | tf_op jit(solution)/shard_map/while/body/eval_jaxpr/qhd,khd->qhk/dot_general | solution.py:40
  388.1 8.3 %fusion.174 = f32[384,4,64]{0,2,1:T(8,128)S(1)} fusion(bf16[2048,4,64]{0,2,1:T(8,128)(2,1)} %bitcast.120, f32[4,2048,384]{2,1,0:T(8,128)} %get-tuple-element.295, f32[384,4]{0,1:T(4,128)S(1)} %select_maximum_fusion.2, pred[384,2048]{0,1:T(8,128)(4,1)S(1)} %compare_and_fusion.2, f32[384,4,64]{0,2,1:T(8,128)S(1)} %get-tuple-element.315, ...), kind=kOutput, calls=%fused_computation.9.clone.1 | convolution fusion | flops 415531008 | bytes 15216641 | tf_op jit(solution)/shard_map/while/body/eval_jaxpr/qhk,khd->qhd/dot_general | solution.py:47
  404.2 8.1 %fusion.171 = (f32[384,4]{0,1:T(4,128)S(1)}, f32[4,2048,384]{2,1,0:T(8,128)}) fusion(pred[384,2048]{0,1:T(8,128)(4,1)S(1)} %compare_and_fusion.2, bf16[2048,4,64]{0,2,1:T(8,128)(2,1)} %bitcast.119, bf16[384,4,64]{0,2,1:T(8,128)(2,1)S(1)} %get-tuple-element.334), kind=kOutput, calls=%fused_computation.4.clone.1 | convolution fusion | flops 412088832 | bytes 14620672 | tf_op jit(solution)/shard_map/while/body/eval_jaxpr/qhd,khd->qhk/dot_general | solution.py:40
  420.9 8.3 %fusion.174 = f32[384,4,64]{0,2,1:T(8,128)S(1)} fusion(bf16[2048,4,64]{0,2,1:T(8,128)(2,1)} %bitcast.120, f32[4,2048,384]{2,1,0:T(8,128)} %get-tuple-element.295, f32[384,4]{0,1:T(4,128)S(1)} %select_maximum_fusion.2, pred[384,2048]{0,1:T(8,128)(4,1)S(1)} %compare_and_fusion.2, f32[384,4,64]{0,2,1:T(8,128)S(1)} %get-tuple-element.315, ...), kind=kOutput, calls=%fused_computation.9.clone.1 | convolution fusion | flops 415531008 | bytes 15216641 | tf_op jit(solution)/shard_map/while/body/eval_jaxpr/qhk,khd->qhd/dot_general | solution.py:47
  432.0 7.6 %all_gather.21 = bf16[2,64,1024]{2,1,0:T(8,128)(2,1)} all-gather(bf16[2,64,256]{2,1,0:T(8,128)(2,1)S(1)} %copy-done.5), channel_id=1, replica_groups=mesh['blk'=32,'head'=4] {'head'}, dimensions={2}, use_global_device_ids=true | all-gather | bytes 327680 | tf_op jit(solution)/shard_map/all_gather | solution.py:190
  457.0 85.6 %all-to-all-done = bf16[2,32,192,256]{3,2,0,1:T(8,128)(2,1)} async-done(((bf16[2,32,192,256]{3,2,0,1:T(8,128)(2,1)}), bf16[2,32,192,256]{3,2,0,1:T(8,128)(2,1)}, u32[]{:S(2)}, u32[]{:S(2)}) %all-to-all-start) | async-done | bytes 6291488 | tf_op jit(solution)/shard_map/all_to_all | solution.py:167
  549.3 62.4 %all-gather.6.cloned.1.call-done = bf16[2,2048,1024]{2,1,0:T(8,128)(2,1)} async-done(((bf16[2,64,1024]{2,1,0:T(8,128)(2,1)}), bf16[2,2048,1024]{2,1,0:T(8,128)(2,1)}) %all-gather.6.cloned.1.call-update) | async-done | bytes 8388624 | tf_op jit(solution)/shard_map/all_gather | solution.py:191
  639.7 9.5 %fusion.41 = bf16[96,16,64]{0,2,1:T(8,128)(2,1)S(1)} fusion(bf16[2048,16,64]{0,2,1:T(8,128)(2,1)} %bitcast.125, f32[16,96,2048]{2,1,0:T(8,128)} %copy-done.1, f32[96,16]{0,1:T(8,128)S(1)} %broadcast_maximum_fusion, pred[96,2048]{1,0:T(8,128)(4,1)S(1)} %broadcast_compare_fusion, f32[96,16]{0,1:T(8,128)S(1)} %get-tuple-element.203, ...), kind=kOutput, calls=%fused_computation.60 | convolution fusion | flops 415531008 | bytes 17188864 | tf_op jit(solution)/shard_map/while/body/eval_jaxpr/qhk,khd->qhd/dot_general | solution.py:47
  650.1 10.2 %fusion.142 = (f32[96]{0:T(128)S(1)}, f32[96,1024]{1,0:T(8,128)S(1)}) fusion(f32[96]{0:T(128)S(1)} %add_rsqrt_fusion.1, f32[96,1024]{1,0:T(8,128)S(1)} %get-tuple-element.211, f32[96]{0:T(128)S(1)} %broadcast_multiply_fusion.2, bf16[4096,1024]{1,0:T(8,128)(2,1)} %param.24, bf16[1024,4096]{1,0:T(8,128)(2,1)} %param.23), kind=kOutput, calls=%fused_computation.204 | convolution fusion | flops 1636859776 | bytes 17564800 | tf_op jit(solution)/shard_map/dot_general | solution.py:212
  661.4 8.7 %all_gather.23 = bf16[384,1024]{1,0:T(8,128)(2,1)S(1)} all-gather(bf16[96,1024]{1,0:T(8,128)(2,1)S(1)} %get-tuple-element.183), channel_id=1, replica_groups=mesh['blk'=32,'head'=4] {'head'}, dimensions={0}, use_global_device_ids=true | all-gather | bytes 983040 | tf_op jit(solution)/shard_map/all_gather | solution.py:214
  (142 shorter events, 158.9 us)
Async XLA Ops:
  7.2 642.1 %copy-start = (bf16[1024,1024]{1,0:T(8,128)(2,1)S(1)}, bf16[1024,1024]{1,0:T(8,128)(2,1)}, u32[]{:S(2)}) copy-start(bf16[1024,1024]{1,0:T(8,128)(2,1)} %param.22) | copy-start | bytes 6291460
  7.2 116.1 %all-gather.8.cloned.1.call-start = ((), (), s32[]{:S(2)}) async-start(), calls=%async_computation.4 | async-start | bytes 6488064 | tf_op jit(solution)/shard_map/all_gather | solution.py:137
  17.9 4.9 copy-start.8
  17.9 5.1 copy-start.6
  20.4 0.8 copy-start.4
  22.0 201.9 %all-gather.10.cloned.1.call-start = ((), (), s32[]{:S(2)}) async-start(), calls=%async_computation.5 | async-start | bytes 6488064 | tf_op jit(solution)/shard_map/all_gather | solution.py:138
  22.8 521.7 %reduce-scatter.2.cloned.1.call-start = ((), (), s32[]{:S(2)}) async-start(), calls=%async_computation.2 | async-start | bytes 1966080 | tf_op jit(solution)/shard_map/reduce_scatter | solution.py:177
  429.2 2.8 copy-start.5
  429.3 10.4 %slice-start = ((bf16[3,384,256]{1,2,0:T(8,128)(2,1)}), bf16[2,384,256]{1,2,0:T(8,128)(2,1)S(1)}, s32[]{:S(2)}) async-start(bf16[3,384,256]{1,2,0:T(8,128)(2,1)} %copy-done.4), calls=%async_computation.6 | async-start | bytes 786432 | tf_op jit(solution)/shard_map/slice | solution.py:156
  432.0 179.7 %all-gather.6.cloned.1.call-start = ((), (), s32[]{:S(2)}) async-start(), calls=%async_computation.3 | async-start | bytes 8650752 | tf_op jit(solution)/shard_map/all_gather | solution.py:191
  445.2 11.3 %copy-start.9 = (s32[9]{0:T(128)S(1)}, s32[9]{0:T(128)}, u32[]{:S(2)}) copy-start(s32[9]{0:T(128)} %param.17) | copy-start | bytes 112
  445.2 99.3 %copy-start.3 = (bf16[96,1024]{1,0:T(8,128)(2,1)S(1)}, bf16[96,1024]{1,0:T(8,128)(2,1)}, u32[]{:S(2)}) copy-start(bf16[96,1024]{1,0:T(8,128)(2,1)} %param.14) | copy-start | bytes 589828
  445.2 97.5 %all-to-all-start = ((bf16[2,32,192,256]{3,2,0,1:T(8,128)(2,1)}), bf16[2,32,192,256]{3,2,0,1:T(8,128)(2,1)}, u32[]{:S(2)}, u32[]{:S(2)}) async-start(bf16[2,32,192,256]{3,2,0,1:T(8,128)(2,1)} %select_select_fusion), calls=%async_computation.1 | async-start | bytes 12582912 | tf_op jit(solution)/shard_map/all_to_all | solution.py:167
  628.7 4.6 copy-start.1
  639.7 9.5 %copy-start.2 = (f32[96,1024]{1,0:T(8,128)S(1)}, f32[96,1024]{1,0:T(8,128)}, u32[]{:S(2)}) copy-start(f32[96,1024]{1,0:T(8,128)} %reduce-scatter.2.cloned.1.call-done) | copy-start | bytes 1179652
  660.3 9.8 %copy-start.7 = (bf16[3,1024,256]{2,1,0:T(8,128)(2,1)S(1)}, bf16[3,1024,256]{2,1,0:T(8,128)(2,1)}, u32[]{:S(2)}) copy-start(bf16[3,1024,256]{2,1,0:T(8,128)(2,1)} %param.25) | copy-start | bytes 4718596
Sparse Core Ops, SparseCore 0:
  22.2 101.0 all-gather.7
  126.6 97.2 all-gather.9
  432.1 22.4 reduce-scatter.1
  457.6 154.0 all-gather.5
where the time goes:
time: 681 us; the launch traced here: 678 us
  waiting for transfers between devices  339 us (50%)
  matrix products  132 us (19%)
  local copies, waits for them, and re-layouts  94.2 us (14%)
  other arithmetic  61.5 us (9%)
  blocking collectives  27.1 us (4%)
  between operations  19.3 us (3%)
    all_gather x1, waiting for transfers between devices, on_device(): lax.all_gather(projected[1], 'blk', axis=0, tiled=True)  97.8 us
    all_gather x1, waiting for transfers between devices, on_device(): lax.all_gather(projected[2], 'blk', axis=0, tiled=True)  92 us
    all_to_all x1, waiting for transfers between devices, on_device(): lax.all_to_all(outgoing, 'blk', split_axis=1, concat_axis=1, tiled=True)  85.6 us
    all_gather x1, waiting for transfers between devices, on_device(): shards = lax.all_gather(widened, 'blk', axis=1, tiled=True)  62.4 us
    dot_general x7, matrix products, online_update(): jnp.einsum('qhk,khd->qhd', weights.astype(jnp.bfloat16), value_split, pre...  59.2 us
    dot_general x7, matrix products, online_update(): jnp.einsum('qhd,khd->qhk', queries, key_split, preferred_element_type=jnp...  52.9 us
    dynamic_slice x24, local copies, waits for them, and re-layouts, sweep(): lax.scan(advance, carried, (key_blocks, value_blocks, place_blocks, group...  51.5 us
    reduce_sum x7, other arithmetic, online_update(): totals = totals * factor + jnp.sum(weights, axis=2)  40.9 us
  transfers between devices with their start and end apart: 5, of which 4 were waited for; matrix products, arithmetic and copies ran while one was open for 4% of the time, Pallas kernels for 0%

commit v1 on v0

--- a/solution.py
+++ b/solution.py
@@ -118,30 +118,27 @@
     group_width = w_qkv.shape[2]
     head_width = model_width // HEADS
     group_heads = group_width // head_width
+    member = lax.axis_index("head")
+    cycle_index = lax.axis_index("blk")
+    encoder = lax.all_gather(enc_kv, "blk", axis=1, tiled=True)
     gathered = lax.all_gather(tokens, "head", axis=0, tiled=True)
     projected = jnp.einsum(
         "td,cde->cte", gathered, w_qkv, preferred_element_type=jnp.float32
     ).astype(jnp.bfloat16)
-    cycle_index = lax.axis_index("blk")
     block_start = cycle_index * block_rows
     query_places = position_of(
         block_order, block_start + jnp.arange(block_rows, dtype=jnp.int32), halfway
     )
     query_groups = group_of(query_places, request_lengths)
     queries = projected[0].reshape(block_rows, group_heads, head_width)
-    start_state = empty_state(block_rows, group_heads, head_width)
     slots = jnp.arange(2 * cycle_size, dtype=jnp.int32)
     holders = jnp.sum(jnp.where(block_order[:, None] == slots[None, :], slots[:, None], 0), axis=0)
-    start_carry = (start_state, jnp.zeros((1,), jnp.bfloat16))
-    shards = (
-        lax.all_gather(projected[1], "blk", axis=0, tiled=True),
-        lax.all_gather(projected[2], "blk", axis=0, tiled=True),
-    )
-    shard_length = shards[0].shape[0]
+    shards = lax.all_gather(projected[1:], "blk", axis=1, tiled=True)
+    shard_length = shards.shape[1]
     key_places = position_of(block_order, jnp.arange(shard_length, dtype=jnp.int32), halfway)
     key_groups = group_of(key_places, request_lengths)
     final_state = sweep(
-        start_carry[0],
+        empty_state(block_rows, group_heads, head_width),
         queries,
         shards[0],
         shards[1],
@@ -151,26 +148,12 @@
         query_groups,
     )
     attended = finish(final_state)
-    pair = lax.dynamic_slice_in_dim(block_order, 2 * cycle_index, 2, 0)
-    targets = pair // 2
-    halves = projected[1:].reshape(2, 2, halfway, group_width)
-    cycle_slots = jnp.arange(cycle_size, dtype=jnp.int32)
-    outgoing = jnp.where(
-        (cycle_slots == targets[0])[None, :, None, None],
-        halves[:, 0][:, None],
-        jnp.where(
-            (cycle_slots == targets[1])[None, :, None, None],
-            halves[:, 1][:, None],
-            jnp.zeros((), jnp.bfloat16),
-        ),
-    )
-    incoming = lax.all_to_all(outgoing, "blk", split_axis=1, concat_axis=1, tiled=True)
-    first_source = lax.dynamic_index_in_dim(holders, 2 * cycle_index, 0, keepdims=False) // 2
-    second_source = lax.dynamic_index_in_dim(holders, 2 * cycle_index + 1, 0, keepdims=False) // 2
+    first_holder = lax.dynamic_index_in_dim(holders, 2 * cycle_index, 0, keepdims=False)
+    second_holder = lax.dynamic_index_in_dim(holders, 2 * cycle_index + 1, 0, keepdims=False)
     cache = jnp.concatenate(
         [
-            lax.dynamic_index_in_dim(incoming, first_source, 1, keepdims=False),
-            lax.dynamic_index_in_dim(incoming, second_source, 1, keepdims=False),
+            lax.dynamic_slice_in_dim(shards, first_holder * halfway, halfway, 1),
+            lax.dynamic_slice_in_dim(shards, second_holder * halfway, halfway, 1),
         ],
         axis=1,
     )
@@ -182,27 +165,29 @@
     )
     hidden = normalize(mixed + tokens.astype(jnp.float32))
     hidden_b = hidden.astype(jnp.bfloat16)
-    member = lax.axis_index("head")
-    own_places = lax.dynamic_slice_in_dim(query_places, member * rows_here, rows_here, 0)
-    own_groups = group_of(own_places, request_lengths)
-    cross_query = jnp.dot(hidden_b, w_cq, preferred_element_type=jnp.float32).astype(jnp.bfloat16)
-    cross_split = cross_query.reshape(rows_here, HEADS, head_width)
-    widened = lax.all_gather(enc_kv, "head", axis=2, tiled=True)
-    shards = lax.all_gather(widened, "blk", axis=1, tiled=True)
-    shard_length = shards.shape[1]
-    encoder_groups = group_of(jnp.arange(shard_length, dtype=jnp.int32), enc_lengths)
-    crossed = finish(
+    block_hidden = lax.all_gather(hidden_b, "head", axis=0, tiled=True)
+    w_cq_group = lax.dynamic_slice_in_dim(w_cq, member * group_width, group_width, 1)
+    cross_query = jnp.dot(
+        block_hidden, w_cq_group, preferred_element_type=jnp.float32
+    ).astype(jnp.bfloat16)
+    cross_split = cross_query.reshape(block_rows, group_heads, head_width)
+    encoder_groups = group_of(jnp.arange(encoder.shape[1], dtype=jnp.int32), enc_lengths)
+    crossed_group = finish(
         sweep(
-            empty_state(rows_here, HEADS, head_width),
+            empty_state(block_rows, group_heads, head_width),
             cross_split,
-            shards[0],
-            shards[1],
+            encoder[0],
+            encoder[1],
             None,
             encoder_groups,
             None,
-            own_groups,
+            query_groups,
         )
     )
+    exchanged = lax.all_to_all(
+        crossed_group.reshape(group_size, rows_here, group_width), "head", 0, 0, tiled=True
+    )
+    crossed = exchanged.transpose(1, 0, 2).reshape(rows_here, model_width)
     summed = jnp.dot(crossed, w_co, preferred_element_type=jnp.float32)
     second = normalize(summed + hidden)
     second_b = second.astype(jnp.bfloat16)

time: 681 us -> 410 us (0.60)
  waiting for transfers between devices: 339 us -> 155 us
  matrix products: 132 us -> 71.2 us
  other arithmetic: 61.5 us -> 41.5 us
    all_gather x3 -> x2, waiting for transfers between devices: 252 us -> 140 us  [the longest x1 140 us: on_device(): shards = lax.all_gather(projected[1:], 'blk', axis=1, tiled=True)]
    all_to_all x1, waiting for transfers between devices: 85.6 us -> 1.98 us  [on_device(): lax.all_to_all(crossed_group.reshape(group_size, rows_here, group_width),...]
    dot_general x7, matrix products: 59.2 us -> 28.1 us  [online_update(): jnp.einsum('qhk,khd->qhd', weights.astype(jnp.bfloat16), value_split, pre...]
    dot_general x7, matrix products: 52.9 us -> 24 us  [online_update(): jnp.einsum('qhd,khd->qhk', queries, key_split, preferred_element_type=jnp...]
    reduce_sum x7, other arithmetic: 40.9 us -> 19.9 us  [online_update(): totals = totals * factor + jnp.sum(weights, axis=2)]
    all_gather x2 -> x0, local copies, waits for them, and re-layouts: 17.3 us -> none  [the longest x1 8.68 us: on_device(): lax.all_gather(projected[1], 'blk', axis=0, tiled=True)]
    slice x1 -> x2, local copies, waits for them, and re-layouts: 6.49 us -> 19.2 us  [on_device(): shards[1]]
    reduce_scatter x1, waiting for transfers between devices: 0.01 us -> 11.5 us  [on_device(): lax.psum_scatter(jnp.dot(attended, w_out, preferred_element_type=jnp.floa...]
  transfers between devices with their start and end apart: 5 -> 4, of which waited for: 4 -> 3; matrix products, arithmetic and copies ran while one was open for 4% -> 41% of each run, Pallas kernels for 0% -> 0%
where the time goes in v1:
time: 410 us; the launch traced here: 408 us
  waiting for transfers between devices  155 us (38%)
  local copies, waits for them, and re-layouts  93.1 us (23%)
  matrix products  71.2 us (17%)
  other arithmetic  41.5 us (10%)
  blocking collectives  28.3 us (7%)
  between operations  15.4 us (4%)
    all_gather x1, waiting for transfers between devices, on_device(): shards = lax.all_gather(projected[1:], 'blk', axis=1, tiled=True)  140 us
    dynamic_slice x24, local copies, waits for them, and re-layouts, sweep(): lax.scan(advance, carried, (key_blocks, value_blocks, place_blocks, group...  50.8 us
    dot_general x7, matrix products, online_update(): jnp.einsum('qhk,khd->qhd', weights.astype(jnp.bfloat16), value_split, pre...  28.1 us
    dot_general x7, matrix products, online_update(): jnp.einsum('qhd,khd->qhk', queries, key_split, preferred_element_type=jnp...  24 us
    reduce_sum x7, other arithmetic, online_update(): totals = totals * factor + jnp.sum(weights, axis=2)  19.9 us
    slice x2, local copies, waits for them, and re-layouts, on_device(): shards[1]  19.2 us
    and x6, other arithmetic, advance(): visible = visible & (place_block[None, :] <= query_places[:, None])  12.6 us
    reduce_scatter x1, waiting for transfers between devices, on_device(): lax.psum_scatter(jnp.dot(attended, w_out, preferred_element_type=jnp.floa...  11.5 us
  transfers between devices with their start and end apart: 4, of which 3 were waited for; matrix products, arithmetic and copies ran while one was open for 41% of the time, Pallas kernels for 0%

profile of v1, /device:TPU:1, one launch (start us, length us, event | category | flops | bytes accessed | tf_op | source)
XLA Modules:
  0.0 408.1 jit_solution(6524547494667970127)
XLA Ops:
  7.2 10.7 %all_gather.15 = bf16[384,1024]{1,0:T(8,128)(2,1)S(1)} all-gather(bf16[96,1024]{1,0:T(8,128)(2,1)} %param.14), channel_id=1, replica_groups=mesh['blk'=32,'head'=4] {'head'}, dimensions={0}, use_global_device_ids=true | all-gather | bytes 983040 | tf_op jit(solution)/shard_map/all_gather | solution.py:124
  25.7 140.3 %all-gather.3.cloned.1.call-done = bf16[2,12288,256]{1,2,0:T(8,128)(2,1)} async-done(((bf16[2,384,256]{1,2,0:T(8,128)(2,1)}), bf16[2,12288,256]{1,2,0:T(8,128)(2,1)}) %all-gather.3.cloned.1.call-update) | async-done | bytes 12582928 | tf_op jit(solution)/shard_map/all_gather | solution.py:136
  166.0 10.5 %fusion.137 = (bf16[1,12288,256]{1,2,0:T(8,128)(2,1)}, bf16[1,12288,256]{1,2,0:T(8,128)(2,1)}) fusion(bf16[2,12288,256]{1,2,0:T(8,128)(2,1)} %all-gather.3.cloned.1.call-done), kind=kLoop, calls=%fused_computation.189 | loop fusion | bytes 25165824 | tf_op jit(solution)/shard_map/slice | solution.py:144
  176.5 8.7 %copy.46 = bf16[1,12288,256]{2,1,0:T(8,128)(2,1)} copy(bf16[1,12288,256]{1,2,0:T(8,128)(2,1)} %get-tuple-element.216) | data formatting | bytes 12582912 | tf_op jit(solution)/shard_map/slice | solution.py:144
  185.2 8.7 %copy.45 = bf16[1,12288,256]{2,1,0:T(8,128)(2,1)} copy(bf16[1,12288,256]{1,2,0:T(8,128)(2,1)} %get-tuple-element.217) | data formatting | bytes 12582912 | tf_op jit(solution)/shard_map/slice | solution.py:143
  193.9 123.7 %while.3 = (s32[]{:T(128)}, f32[384,4]{0,1:T(4,128)S(1)}, f32[384,4]{0,1:T(4,128)S(1)}, f32[384,4,64]{0,2,1:T(8,128)S(1)}, s32[6,2048]{1,0:T(8,128)}, /*index=5*...) while((s32[]{:T(128)}, f32[384,4]{0,1:T(4,128)S(1)}, ...), condition=%wide.region_10.11_spmd.clone, body=%wide.region_7.10_spmd.clone.sunk | while | flops 842571264 | bytes 56708272 | solution.py:79
  204.6 3.6 fusion.170
  211.0 3.6 fusion.173
  225.2 3.6 fusion.170
  231.6 3.6 fusion.173
  245.8 3.6 fusion.170
  252.2 3.6 fusion.173
  266.4 3.6 fusion.170
  272.8 3.6 fusion.173
  287.0 3.6 fusion.170
  293.4 3.6 fusion.173
  307.6 3.6 fusion.170
  314.0 3.6 fusion.173
  331.0 11.5 %reduce-scatter.2.cloned.1.call-done = f32[96,1024]{1,0:T(8,128)} async-done(((f32[384,1024]{1,0:T(8,128)}), f32[96,1024]{1,0:T(8,128)}) %reduce-scatter.2.cloned.1.call-update) | async-done | bytes 393232 | tf_op jit(solution)/shard_map/reduce_scatter | solution.py:160
  346.1 8.9 %all_gather.17 = bf16[384,1024]{1,0:T(8,128)(2,1)S(1)} all-gather(bf16[96,1024]{1,0:T(8,128)(2,1)S(1)} %multiply_convert_fusion.1), channel_id=1, replica_groups=mesh['blk'=32,'head'=4] {'head'}, dimensions={0}, use_global_device_ids=true | all-gather | bytes 983040 | tf_op jit(solution)/shard_map/all_gather | solution.py:168
  363.7 6.4 %fusion.41 = bf16[384,4,64]{0,2,1:T(8,128)(2,1)S(1)} fusion(bf16[2048,4,64]{0,2,1:T(8,128)(2,1)S(1)} %bitcast.118, f32[4,384,2048]{2,1,0:T(8,128)} %copy-done.1, f32[384,4]{0,1:T(4,128)S(1)} %broadcast_maximum_fusion, pred[384,2048]{1,0:T(8,128)(4,1)S(1)} %broadcast_compare_fusion, f32[384,4]{0,1:T(4,128)S(1)} %get-tuple-element.223, ...), kind=kOutput, calls=%fused_computation.60 | convolution fusion | flops 415531008 | bytes 14632960 | tf_op jit(solution)/shard_map/while/body/eval_jaxpr/qhk,khd->qhd/dot_general | solution.py:47
  371.2 3.5 all-to-all-start
  380.0 10.0 %fusion.141 = (f32[96]{0:T(128)S(1)}, f32[96,1024]{1,0:T(8,128)S(1)}) fusion(f32[96]{0:T(128)S(1)} %add_rsqrt_fusion.1, f32[96,1024]{1,0:T(8,128)S(1)} %get-tuple-element.229, f32[96]{0:T(128)S(1)} %broadcast_multiply_fusion.2, bf16[4096,1024]{1,0:T(8,128)(2,1)} %param.24, bf16[1024,4096]{1,0:T(8,128)(2,1)} %param.23), kind=kOutput, calls=%fused_computation.193 | convolution fusion | flops 1636859776 | bytes 17564800 | tf_op jit(solution)/shard_map/dot_general | solution.py:197
  391.1 8.7 %all_gather.19 = bf16[384,1024]{1,0:T(8,128)(2,1)S(1)} all-gather(bf16[96,1024]{1,0:T(8,128)(2,1)S(1)} %get-tuple-element.206), channel_id=1, replica_groups=mesh['blk'=32,'head'=4] {'head'}, dimensions={0}, use_global_device_ids=true | all-gather | bytes 983040 | tf_op jit(solution)/shard_map/all_gather | solution.py:199
  (156 shorter events, 121.1 us)
Async XLA Ops:
  7.2 372.0 %copy-start = (bf16[1024,1024]{1,0:T(8,128)(2,1)S(1)}, bf16[1024,1024]{1,0:T(8,128)(2,1)}, u32[]{:S(2)}) copy-start(bf16[1024,1024]{1,0:T(8,128)(2,1)} %param.22) | copy-start | bytes 6291460
  7.2 158.8 %all-gather.3.cloned.1.call-start = ((), (), s32[]{:S(2)}) async-start(), calls=%async_computation.2 | async-start | bytes 12976128 | tf_op jit(solution)/shard_map/all_gather | solution.py:136
  20.4 156.2 %copy-start.3 = (bf16[3,384,256]{1,2,0:T(8,128)(2,1)}, bf16[3,384,256]{1,2,0:T(8,128)(2,1)S(1)}, u32[]{:S(2)}) copy-start(bf16[3,384,256]{1,2,0:T(8,128)(2,1)S(1)} %fusion.31) | copy-start | bytes 1769476
  20.4 1.9 copy-start.10
  21.2 302.1 %all-gather.5.cloned.1.call-start = ((), (), s32[]{:S(2)}) async-start(), calls=%async_computation.4 | async-start | bytes 2162688 | tf_op jit(solution)/shard_map/all_gather | solution.py:123
  22.0 320.5 %reduce-scatter.2.cloned.1.call-start = ((), (), s32[]{:S(2)}) async-start(), calls=%async_computation.3 | async-start | bytes 1966080 | tf_op jit(solution)/shard_map/reduce_scatter | solution.py:160
  185.2 8.7 %slice-start = ((bf16[3,384,256]{1,2,0:T(8,128)(2,1)}), bf16[1,384,256]{1,2,0:T(8,128)(2,1)S(1)}, s32[]{:S(2)}) async-start(bf16[3,384,256]{1,2,0:T(8,128)(2,1)} %copy-done.3), calls=%async_computation.5 | async-start | bytes 393216 | tf_op jit(solution)/shard_map/slice | solution.py:133
  185.2 8.7 %copy-start.8 = (f32[384,4,64]{0,2,1:T(8,128)S(1)}, f32[384,4,64]{0,2,1:T(8,128)}, u32[]{:S(2)}) copy-start(f32[384,4,64]{0,2,1:T(8,128)} %custom-call.2) | copy-start | bytes 1179652
  208.1 2.8 copy-start.2
  228.8 2.8 copy-start.2
  249.4 2.8 copy-start.2
  270.0 2.8 copy-start.2
  290.6 2.8 copy-start.2
  311.2 2.8 copy-start.2
  317.7 2.7 copy-start.11
  317.7 4.7 %copy-start.14 = (s32[9]{0:T(128)S(1)}, s32[9]{0:T(128)}, u32[]{:S(2)}) copy-start(s32[9]{0:T(128)} %param.17) | copy-start | bytes 112
  317.7 5.0 %copy-start.9 = (s32[384]{0:T(512)S(1)}, s32[384]{0:T(512)}, u32[]{:S(2)}) copy-start(s32[384]{0:T(512)} %get-tuple-element.365) | copy-start | bytes 4612
  328.7 13.8 %copy-start.5 = (bf16[96,1024]{1,0:T(8,128)(2,1)S(1)}, bf16[96,1024]{1,0:T(8,128)(2,1)}, u32[]{:S(2)}) copy-start(bf16[96,1024]{1,0:T(8,128)(2,1)} %param.14) | copy-start | bytes 589828
  344.9 11.7 %copy-start.6 = (bf16[1,2048,256]{1,2,0:T(8,128)(2,1)S(1)}, bf16[1,2048,256]{1,2,0:T(8,128)(2,1)}, u32[]{:S(2)}) copy-start(bf16[1,2048,256]{1,2,0:T(8,128)(2,1)} %copy.49) | copy-start | bytes 3145732
  359.1 4.5 %copy-start.1 = (f32[4,384,2048]{2,1,0:T(8,128)}, f32[4,384,2048]{2,1,0:T(8,128)S(1)}, u32[]{:S(2)}) copy-start(f32[4,384,2048]{2,1,0:T(8,128)S(1)} %get-tuple-element.227) | copy-start | bytes 37748740
  359.1 4.5 %copy-start.7 = (bf16[1,2048,256]{1,2,0:T(8,128)(2,1)S(1)}, bf16[1,2048,256]{1,2,0:T(8,128)(2,1)}, u32[]{:S(2)}) copy-start(bf16[1,2048,256]{1,2,0:T(8,128)(2,1)} %copy.50) | copy-start | bytes 3145732
  371.2 8.0 %all-to-all-start = ((bf16[4,96,256]{2,1,0:T(8,128)(2,1)}), bf16[4,96,256]{2,1,0:T(8,128)(2,1)S(1)}, u32[]{:S(2)}, u32[]{:S(2)}) async-start(bf16[4,96,256]{2,1,0:T(8,128)(2,1)} %copy.51), calls=%async_computation.1 | async-start | bytes 393216 | tf_op jit(solution)/shard_map/all_to_all | solution.py:187
  374.6 4.5 %copy-start.4 = (f32[96,1024]{1,0:T(8,128)S(1)}, f32[96,1024]{1,0:T(8,128)}, u32[]{:S(2)}) copy-start(f32[96,1024]{1,0:T(8,128)} %reduce-scatter.2.cloned.1.call-done) | copy-start | bytes 1179652
  390.0 9.8 %copy-start.12 = (bf16[3,1024,256]{2,1,0:T(8,128)(2,1)S(1)}, bf16[3,1024,256]{2,1,0:T(8,128)(2,1)}, u32[]{:S(2)}) copy-start(bf16[3,1024,256]{2,1,0:T(8,128)(2,1)} %param.25) | copy-start | bytes 4718596
  (1 other events, 1.7 us)
Sparse Core Ops, SparseCore 0:
  21.3 144.6 all-gather.2
  169.0 68.1 all-gather.4
  320.5 21.8 reduce-scatter.1

commit v2 on v1

--- a/solution.py
+++ b/solution.py
@@ -1,8 +1,11 @@
+import functools
 import math
 
 import jax
 import jax.numpy as jnp
 from jax import lax
+from jax.experimental import pallas as pl
+from jax.experimental.pallas import tpu as pltpu
 from jax.sharding import PartitionSpec as P
 
 HEADS = 16
@@ -93,6 +96,118 @@
 def finish(carried):
     maxima, totals, running = carried
     return (running / totals[:, :, None]).reshape(running.shape[0], -1).astype(jnp.bfloat16)
+
+
+def flash_kernel(
+    steps_ref, sources_ref, bases_ref, q_ref, low_ref, high_ref, k_hbm, v_hbm, o_ref,
+    kbuf, vbuf, sem, qm_sc, m_sc, l_sc, acc_sc, *, max_steps, heads, head_width
+):
+    half = pl.program_id(0)
+    count = steps_ref[half]
+    tile = kbuf.shape[1] // 2
+    width = kbuf.shape[2]
+
+    def copies(step, slot):
+        result = []
+        for j in range(2):
+            source = pl.multiple_of(sources_ref[(half * max_steps + step) * 2 + j], tile)
+            window = pl.ds(j * tile, tile)
+            result.append(pltpu.make_async_copy(
+                k_hbm.at[pl.ds(source, tile)], kbuf.at[slot, window], sem.at[0, slot, j]))
+            result.append(pltpu.make_async_copy(
+                v_hbm.at[pl.ds(source, tile)], vbuf.at[slot, window], sem.at[1, slot, j]))
+        return result
+
+    for copy in copies(0, 0):
+        copy.start()
+    column_head = lax.broadcasted_iota(jnp.int32, (1, width), 1) // head_width
+    q = q_ref[0]
+    for h in range(heads):
+        qm_sc[h] = jnp.where(column_head == h, q, jnp.zeros_like(q))
+    m_sc[...] = jnp.full(m_sc.shape, NEGATIVE, jnp.float32)
+    l_sc[...] = jnp.zeros(l_sc.shape, jnp.float32)
+    acc_sc[...] = jnp.zeros(acc_sc.shape, jnp.float32)
+    low = low_ref[0]
+    high = high_ref[0]
+
+    def body(step, carry):
+        slot = step % 2
+        for copy in copies(step, slot):
+            copy.wait()
+
+        @pl.when(step + 1 < count)
+        def _():
+            for copy in copies(step + 1, 1 - slot):
+                copy.start()
+
+        base = bases_ref[half * max_steps + step]
+        places = base + lax.broadcasted_iota(jnp.int32, (1, 2 * tile), 1)
+        visible = (places >= low) & (places <= high)
+        keys = kbuf[slot]
+        values = vbuf[slot]
+        for h in range(heads):
+            scores = lax.dot_general(
+                qm_sc[h], keys, (((1,), (1,)), ((), ())), preferred_element_type=jnp.float32
+            ) * SCALING
+            scores = jnp.where(visible, scores, NEGATIVE)
+            previous = m_sc[h]
+            updated = jnp.maximum(previous, jnp.max(scores, axis=1, keepdims=True))
+            factor = jnp.exp(previous - updated)
+            weights = jnp.exp(scores - updated)
+            l_sc[h] = l_sc[h] * factor + jnp.sum(weights, axis=1, keepdims=True)
+            acc_sc[h] = acc_sc[h] * factor + jnp.dot(
+                weights.astype(jnp.bfloat16), values, preferred_element_type=jnp.float32
+            )
+            m_sc[h] = updated
+        return carry
+
+    lax.fori_loop(0, count, body, 0)
+    out = jnp.zeros(acc_sc.shape[1:], jnp.float32)
+    for h in range(heads):
+        out = jnp.where(column_head == h, acc_sc[h] / l_sc[h], out)
+    o_ref[0] = out.astype(o_ref.dtype)
+
+
+def flash(queries, low, high, keys, values, steps, sources, bases, max_steps, heads):
+    halves, tile, width = queries.shape
+    head_width = width // heads
+    kernel = functools.partial(
+        flash_kernel, max_steps=max_steps, heads=heads, head_width=head_width
+    )
+    row_spec = pl.BlockSpec((1, tile, width), lambda h, *refs: (h, 0, 0))
+    bound_spec = pl.BlockSpec((1, tile, 1), lambda h, *refs: (h, 0, 0))
+    flops = 4 * halves * max_steps * tile * 2 * tile * width * heads
+    return pl.pallas_call(
+        kernel,
+        out_shape=jax.ShapeDtypeStruct(queries.shape, jnp.bfloat16),
+        grid_spec=pltpu.PrefetchScalarGridSpec(
+            num_scalar_prefetch=3,
+            grid=(halves,),
+            in_specs=[
+                row_spec,
+                bound_spec,
+                bound_spec,
+                pl.BlockSpec(memory_space=pl.ANY),
+                pl.BlockSpec(memory_space=pl.ANY),
+            ],
+            out_specs=row_spec,
+            scratch_shapes=[
+                pltpu.VMEM((2, 2 * tile, width), keys.dtype),
+                pltpu.VMEM((2, 2 * tile, width), values.dtype),
+                pltpu.SemaphoreType.DMA((2, 2, 2)),
+                pltpu.VMEM((heads, tile, width), jnp.bfloat16),
+                pltpu.VMEM((heads, tile, 1), jnp.float32),
+                pltpu.VMEM((heads, tile, 1), jnp.float32),
+                pltpu.VMEM((heads, tile, width), jnp.float32),
+            ],
+        ),
+        compiler_params=pltpu.CompilerParams(dimension_semantics=("arbitrary",)),
+        cost_estimate=pl.CostEstimate(
+            flops=flops,
+            transcendentals=halves * max_steps * tile * 2 * tile * heads,
+            bytes_accessed=halves * max_steps * 2 * 2 * tile * width * 2,
+        ),
+    )(steps, sources, bases, queries, low, high, keys, values)
 
 
 def on_device(
@@ -134,20 +249,33 @@
     slots = jnp.arange(2 * cycle_size, dtype=jnp.int32)
     holders = jnp.sum(jnp.where(block_order[:, None] == slots[None, :], slots[:, None], 0), axis=0)
     shards = lax.all_gather(projected[1:], "blk", axis=1, tiled=True)
-    shard_length = shards.shape[1]
-    key_places = position_of(block_order, jnp.arange(shard_length, dtype=jnp.int32), halfway)
-    key_groups = group_of(key_places, request_lengths)
-    final_state = sweep(
-        empty_state(block_rows, group_heads, head_width),
-        queries,
+    ends = jnp.cumsum(request_lengths).astype(jnp.int32)
+    starts = ends - request_lengths
+    pair = lax.dynamic_slice_in_dim(block_order, 2 * cycle_index, 2, 0)
+    first_request = group_of(pair * halfway, request_lengths)
+    low_block = starts[first_request] // halfway
+    self_steps = (pair - low_block) // 2 + 1
+    self_max = cycle_size
+    firsts = jnp.minimum(
+        low_block[:, None] + 2 * jnp.arange(self_max, dtype=jnp.int32)[None, :],
+        2 * cycle_size - 1,
+    )
+    padded_holders = jnp.concatenate([holders, holders[:1]])
+    self_sources = jnp.stack(
+        [padded_holders[firsts], padded_holders[firsts + 1]], axis=-1
+    ) * halfway
+    attended = flash(
+        projected[0].reshape(2, halfway, group_width),
+        starts[query_groups].reshape(2, halfway, 1),
+        query_places.reshape(2, halfway, 1),
         shards[0],
         shards[1],
-        key_places,
-        key_groups,
-        query_places,
-        query_groups,
-    )
-    attended = finish(final_state)
+        self_steps.astype(jnp.int32),
+        self_sources.reshape(-1).astype(jnp.int32),
+        (firsts * halfway).reshape(-1).astype(jnp.int32),
+        self_max,
+        group_heads,
+    ).reshape(block_rows, group_width)
     first_holder = lax.dynamic_index_in_dim(holders, 2 * cycle_index, 0, keepdims=False)
     second_holder = lax.dynamic_index_in_dim(holders, 2 * cycle_index + 1, 0, keepdims=False)
     cache = jnp.concatenate(
@@ -170,20 +298,33 @@
     cross_query = jnp.dot(
         block_hidden, w_cq_group, preferred_element_type=jnp.float32
     ).astype(jnp.bfloat16)
-    cross_split = cross_query.reshape(block_rows, group_heads, head_width)
-    encoder_groups = group_of(jnp.arange(encoder.shape[1], dtype=jnp.int32), enc_lengths)
-    crossed_group = finish(
-        sweep(
-            empty_state(block_rows, group_heads, head_width),
-            cross_split,
-            encoder[0],
-            encoder[1],
-            None,
-            encoder_groups,
-            None,
-            query_groups,
-        )
-    )
+    encoder_rows = encoder.shape[1]
+    cross_max = (encoder_rows + halfway - 1 + 2 * halfway - 1) // (2 * halfway)
+    padded_encoder = jnp.pad(
+        encoder, ((0, 0), (0, cross_max * 2 * halfway + halfway - encoder_rows), (0, 0))
+    )
+    enc_ends = jnp.cumsum(enc_lengths).astype(jnp.int32)
+    enc_starts = enc_ends - enc_lengths
+    edge_groups = query_groups.reshape(2, halfway)
+    cross_base = (enc_starts[edge_groups[:, 0]] // halfway) * halfway
+    cross_steps = (enc_ends[edge_groups[:, -1]] - cross_base + 2 * halfway - 1) // (2 * halfway)
+    cross_firsts = jnp.minimum(
+        cross_base[:, None] + 2 * halfway * jnp.arange(cross_max, dtype=jnp.int32)[None, :],
+        padded_encoder.shape[1] - 2 * halfway,
+    )
+    cross_sources = jnp.stack([cross_firsts, cross_firsts + halfway], axis=-1)
+    crossed_group = flash(
+        cross_query.reshape(2, halfway, group_width),
+        enc_starts[query_groups].reshape(2, halfway, 1),
+        (enc_ends[query_groups] - 1).reshape(2, halfway, 1),
+        padded_encoder[0],
+        padded_encoder[1],
+        cross_steps.astype(jnp.int32),
+        cross_sources.reshape(-1).astype(jnp.int32),
+        cross_firsts.reshape(-1).astype(jnp.int32),
+        cross_max,
+        group_heads,
+    ).reshape(block_rows, group_width)
     exchanged = lax.all_to_all(
         crossed_group.reshape(group_size, rows_here, group_width), "head", 0, 0, tiled=True
     )

time: 410 us -> 314 us (0.77)
  local copies, waits for them, and re-layouts: 93.1 us -> 28.1 us
  matrix products: 71.2 us -> 19.2 us
  Pallas kernels: 0 us -> 19.8 us
  other arithmetic: 41.5 us -> 26.4 us
  waiting for transfers between devices: 155 us -> 170 us
    dot_general x14 -> x0, matrix products: 52.2 us -> none  [the longest x7 28.1 us: online_update(): jnp.einsum('qhk,khd->qhd', weights.astype(jnp.bfloat16), value_split, pre...]
    dynamic_slice x24 -> x0, local copies, waits for them, and re-layouts: 50.8 us -> none  [sweep(): lax.scan(advance, carried, (key_blocks, value_blocks, place_blocks, group...]
    all_gather x1, waiting for transfers between devices: 0.02 us -> 42.7 us  [on_device(): encoder = lax.all_gather(enc_kv, 'blk', axis=1, tiled=True)]
    all_gather x1, waiting for transfers between devices: 140 us -> 102 us  [on_device(): shards = lax.all_gather(projected[1:], 'blk', axis=1, tiled=True)]
    slice x8 -> x1, local copies, waits for them, and re-layouts: 35.6 us -> 0.69 us  [on_device(): projected[0].reshape(2, halfway, group_width)]
    reduce_sum x7 -> x0, other arithmetic: 19.9 us -> none  [online_update(): totals = totals * factor + jnp.sum(weights, axis=2)]
    pallas_call x0 -> x2, Pallas kernels: none -> 19.8 us  [flash(): pl.pallas_call(kernel, out_shape=jax.ShapeDtypeStruct(queries.shape, jnp....]
    squeeze x0 -> x2, local copies, waits for them, and re-layouts: none -> 13.3 us  [the longest x1 10.1 us: on_device(): shards[1]]
  transfers between devices with their start and end apart: 4 -> 4, of which waited for: 3 -> 4; matrix products, arithmetic and copies ran while one was open for 41% -> 17% of each run, Pallas kernels for 0% -> 3%
where the time goes in v2:
time: 314 us; the launch traced here: 310 us
  waiting for transfers between devices  170 us (54%)
  local copies, waits for them, and re-layouts  28.1 us (9%)
  blocking collectives  28.1 us (9%)
  other arithmetic  26.4 us (8%)
  Pallas kernels  19.8 us (6%)
  matrix products  19.2 us (6%)
  between operations  15.2 us (5%)
  starting transfers between devices  3.8 us (1%)
    all_gather x1, waiting for transfers between devices, on_device(): shards = lax.all_gather(projected[1:], 'blk', axis=1, tiled=True)  102 us
    all_gather x1, waiting for transfers between devices, on_device(): encoder = lax.all_gather(enc_kv, 'blk', axis=1, tiled=True)  42.7 us
    reduce_scatter x1, waiting for transfers between devices, on_device(): lax.psum_scatter(jnp.dot(attended, w_out, preferred_element_type=jnp.floa...  22 us
    pallas_call x2, Pallas kernels, flash(): pl.pallas_call(kernel, out_shape=jax.ShapeDtypeStruct(queries.shape, jnp....  19.8 us
    all_gather x1, blocking collectives, on_device(): gathered = lax.all_gather(tokens, 'head', axis=0, tiled=True)  10.7 us
    squeeze x1, local copies, waits for them, and re-layouts, on_device(): shards[1]  10.1 us
    dot_general x1, matrix products, on_device(): jnp.dot(inner, w_down, preferred_element_type=jnp.float32) + second  10 us
    all_gather x1, blocking collectives, on_device(): block_hidden = lax.all_gather(hidden_b, 'head', axis=0, tiled=True)  8.72 us
  transfers between devices with their start and end apart: 4, of which 4 were waited for; matrix products, arithmetic and copies ran while one was open for 17% of the time, Pallas kernels for 3%

profile of v2, /device:TPU:1, one launch (start us, length us, event | category | flops | bytes accessed | tf_op | source)
XLA Modules:
  0.0 310.3 jit_solution(13022322676540537210)
XLA Ops:
  7.2 10.7 %all_gather.15 = bf16[384,1024]{1,0:T(8,128)(2,1)S(1)} all-gather(bf16[96,1024]{1,0:T(8,128)(2,1)} %param.12), channel_id=1, replica_groups=mesh['blk'=32,'head'=4] {'head'}, dimensions={0}, use_global_device_ids=true | all-gather | bytes 983040 | tf_op jit(solution)/shard_map/all_gather | solution.py:239
  17.9 2.2 fusion.12
  31.9 8.7 %select_reduce_fusion.2 = (s32[384]{0:T(512)S(1)}, s32[384]{0:T(512)S(1)}, s32[384,1]{0,1:T(1,128)S(1)}) fusion(s32[]{:T(128)} %bitcast.32, s32[]{:T(128)} %bitcast.33, s32[]{:T(128)} %bitcast.34, s32[]{:T(128)} %bitcast.35, s32[]{:T(128)} %bitcast.36, s32[]{:T(128)} %bitcast.38, s32[]{:T(128)} %bitcast.37, s32[]{:T(128)} %bitcast.29, s32[]{:T(128)} %bitcast.28, ...), kind=kLoop, calls=%fused_computation.125 | loop fusion | flops 8064 | bytes 6200 | tf_op jit(solution)/shard_map/gather | solution.py:319
  40.6 4.3 %select_reduce_fusion.4 = s32[384]{0:T(512)S(1)} fusion(s32[]{:T(128)} %bitcast.10, s32[]{:T(128)} %bitcast.11, s32[]{:T(128)} %bitcast.12, s32[]{:T(128)} %bitcast.13, s32[]{:T(128)} %bitcast.14, s32[]{:T(128)} %bitcast.16, s32[]{:T(128)} %bitcast.15, s32[384,1]{0,1:T(1,128)S(1)} %get-tuple-element.11), kind=kLoop, calls=%fused_computation.127 | loop fusion | flops 4608 | bytes 3100 | tf_op jit(solution)/shard_map/gather | solution.py:269
  44.9 3.7 %select_add_fusion = (s32[384]{0:T(512)S(1)}, s32[384]{0:T(512)S(1)}, s32[384]{0:T(512)S(1)}) fusion(pred[384]{0:T(512)(128)(4,1)S(1)} %get-tuple-element.8, pred[384]{0:T(512)(128)(4,1)S(1)} %get-tuple-element.7, s32[384]{0:T(512)S(1)} %get-tuple-element.5, s32[]{:T(128)} %bitcast.30, s32[]{:T(128)} %bitcast.31, s32[384]{0:T(512)S(1)} %get-tuple-element.6, ...), kind=kLoop, calls=%fused_computation.110 | loop fusion | flops 2688 | bytes 10008 | tf_op jit(solution)/shard_map/sub | solution.py:319
  50.5 101.7 %all-gather.3.cloned.1.call-done = bf16[2,12288,256]{2,1,0:T(8,128)(2,1)} async-done(((bf16[2,384,256]{2,1,0:T(8,128)(2,1)}), bf16[2,12288,256]{2,1,0:T(8,128)(2,1)}) %all-gather.3.cloned.1.call-update) | async-done | bytes 12582928 | tf_op jit(solution)/shard_map/all_gather | solution.py:251
  152.2 10.1 %slice_bitcast_fusion = (bf16[12288,256]{1,0:T(8,128)(2,1)}, bf16[12288,256]{1,0:T(8,128)(2,1)}) fusion(bf16[2,12288,256]{2,1,0:T(8,128)(2,1)} %all-gather.3.cloned.1.call-done), kind=kLoop, calls=%fused_computation.5 | loop fusion | bytes 25165824 | tf_op jit(solution)/shard_map/squeeze | solution.py:272
  162.3 10.0 %shard_map.139 = bf16[2,192,256]{2,1,0:T(8,128)(2,1)} custom-call(s32[2]{0:T(128)} %get-tuple-element.12.steps_ref, s32[128]{0:T(128)} %mul.152.sources_ref, s32[64]{0:T(128)} %mul.155.bases_ref, bf16[2,192,256]{2,1,0:T(8,128)(2,1)} %bitcast.78, s32[2,192,1]{2,1,0:T(8,128)} %reshape.657.low_ref, s32[2,192,1]{2,1,0:T(8,128)} %fusion.47.high_ref, ...), custom_call_target="tpu_custom_call" | custom-call | flops 19327352832 | bytes 25165824 | tf_op jit(solution)/shard_map/pallas_call | solution.py:180
  172.3 2.5 fusion.108
  181.2 42.7 %all-gather.5.cloned.1.call-done = bf16[2,2048,256]{2,1,0:T(8,128)(2,1)} async-done(((bf16[2,64,256]{2,1,0:T(8,128)(2,1)}), bf16[2,2048,256]{2,1,0:T(8,128)(2,1)}) %all-gather.5.cloned.1.call-update) | async-done | bytes 2097168 | tf_op jit(solution)/shard_map/all_gather | solution.py:238
  223.8 3.2 %fusion.11 = (bf16[2496,256]{1,0:T(8,128)(2,1)}, bf16[2496,256]{1,0:T(8,128)(2,1)}) fusion(bf16[2,2048,256]{2,1,0:T(8,128)(2,1)} %all-gather.5.cloned.1.call-done), kind=kLoop, calls=%fused_computation.31 | loop fusion | bytes 4653056 | tf_op jit(solution)/shard_map/squeeze | solution.py:321
  227.0 22.0 %reduce-scatter.2.cloned.1.call-done = f32[96,1024]{1,0:T(8,128)} async-done(((f32[384,1024]{1,0:T(8,128)}), f32[96,1024]{1,0:T(8,128)}) %reduce-scatter.2.cloned.1.call-update) | async-done | bytes 393232 | tf_op jit(solution)/shard_map/reduce_scatter | solution.py:288
  249.0 1.1 fusion.56
  250.2 1.2 multiply_reduce_fusion.2
  251.4 1.1 multiply_convert_fusion.1
  252.5 8.7 %all_gather.17 = bf16[384,1024]{1,0:T(8,128)(2,1)S(1)} all-gather(bf16[96,1024]{1,0:T(8,128)(2,1)S(1)} %multiply_convert_fusion.1), channel_id=1, replica_groups=mesh['blk'=32,'head'=4] {'head'}, dimensions={0}, use_global_device_ids=true | all-gather | bytes 983040 | tf_op jit(solution)/shard_map/all_gather | solution.py:296
  261.3 2.1 convolution_convert_fusion.1
  263.3 9.8 %shard_map.140 = bf16[2,192,256]{2,1,0:T(8,128)(2,1)} custom-call(s32[2]{0:T(128)} %get-tuple-element.16.steps_ref, s32[24]{0:T(128)} %reshape.480.sources_ref, s32[12]{0:T(128)} %min.45.bases_ref, bf16[2,192,256]{2,1,0:T(8,128)(2,1)} %bitcast.80, s32[2,192,1]{2,1,0:T(8,128)} %reshape.658.low_ref, s32[2,192,1]{2,1,0:T(8,128)} %sub.85.high_ref, ...), custom_call_target="tpu_custom_call" | custom-call | flops 3623878656 | bytes 4718592 | tf_op jit(solution)/shard_map/pallas_call | solution.py:180
  273.2 3.7 %all-to-all-start = ((bf16[4,96,256]{2,1,0:T(8,128)(2,1)}), bf16[4,96,256]{2,1,0:T(8,128)(2,1)S(1)}, u32[]{:S(2)}, u32[]{:S(2)}) async-start(bf16[4,96,256]{2,1,0:T(8,128)(2,1)} %bitcast.79), calls=%async_computation.1 | async-start | bytes 393216 | tf_op jit(solution)/shard_map/all_to_all | solution.py:328
  276.9 1.1 constant_dynamic-slice_fusion.1
  278.7 2.6 all-to-all-done
  282.2 10.0 %fusion.107 = (f32[96]{0:T(128)S(1)}, f32[96,1024]{1,0:T(8,128)S(1)}) fusion(f32[96]{0:T(128)S(1)} %add_rsqrt_fusion.1, f32[96,1024]{1,0:T(8,128)S(1)} %get-tuple-element.62, f32[96]{0:T(128)S(1)} %broadcast_multiply_fusion.2, bf16[4096,1024]{1,0:T(8,128)(2,1)} %param.22, bf16[1024,4096]{1,0:T(8,128)(2,1)} %param.21), kind=kOutput, calls=%fused_computation.200 | convolution fusion | flops 1636859776 | bytes 17564800 | tf_op jit(solution)/shard_map/dot_general | solution.py:338
  293.3 8.7 %all_gather.19 = bf16[384,1024]{1,0:T(8,128)(2,1)S(1)} all-gather(bf16[96,1024]{1,0:T(8,128)(2,1)S(1)} %get-tuple-element.9), channel_id=1, replica_groups=mesh['blk'=32,'head'=4] {'head'}, dimensions={0}, use_global_device_ids=true | all-gather | bytes 983040 | tf_op jit(solution)/shard_map/all_gather | solution.py:340
  302.0 1.8 convolution_bitcast_fusion
  (91 shorter events, 21.5 us)
Async XLA Ops:
  7.2 274.1 %copy-start = (bf16[1024,1024]{1,0:T(8,128)(2,1)S(1)}, bf16[1024,1024]{1,0:T(8,128)(2,1)}, u32[]{:S(2)}) copy-start(bf16[1024,1024]{1,0:T(8,128)(2,1)} %param.20) | copy-start | bytes 6291460
  7.2 145.0 %all-gather.3.cloned.1.call-start = ((), (), s32[]{:S(2)}) async-start(), calls=%async_computation.2 | async-start | bytes 12976128 | tf_op jit(solution)/shard_map/all_gather | solution.py:251
  17.9 3.8 %copy-start.6 = (s32[9]{0:T(128)S(1)}, s32[9]{0:T(128)}, u32[]{:S(2)}) copy-start(s32[9]{0:T(128)} %param.14) | copy-start | bytes 112
  17.9 4.1 %copy-start.4 = (s32[64]{0:T(128)S(1)}, s32[64]{0:T(128)}, u32[]{:S(2)}) copy-start(s32[64]{0:T(128)} %param.13) | copy-start | bytes 772
  20.2 4.9 %copy-start.7 = (s32[9]{0:T(128)S(1)}, s32[9]{0:T(128)}, u32[]{:S(2)}) copy-start(s32[9]{0:T(128)} %param.15) | copy-start | bytes 112
  21.0 202.9 %all-gather.5.cloned.1.call-start = ((), (), s32[]{:S(2)}) async-start(), calls=%async_computation.4 | async-start | bytes 2162688 | tf_op jit(solution)/shard_map/all_gather | solution.py:238
  21.7 227.3 %reduce-scatter.2.cloned.1.call-start = ((), (), s32[]{:S(2)}) async-start(), calls=%async_computation.3 | async-start | bytes 1966080 | tf_op jit(solution)/shard_map/reduce_scatter | solution.py:288
  162.3 10.0 %copy-start.3 = (bf16[256,1024]{1,0:T(8,128)(2,1)S(1)}, bf16[256,1024]{1,0:T(8,128)(2,1)}, u32[]{:S(2)}) copy-start(bf16[256,1024]{1,0:T(8,128)(2,1)} %param.17) | copy-start | bytes 1572868
  181.2 67.9 %copy-start.2 = (bf16[96,1024]{1,0:T(8,128)(2,1)S(1)}, bf16[96,1024]{1,0:T(8,128)(2,1)}, u32[]{:S(2)}) copy-start(bf16[96,1024]{1,0:T(8,128)(2,1)} %param.12) | copy-start | bytes 589828
  273.2 8.1 %copy-start.1 = (f32[96,1024]{1,0:T(8,128)S(1)}, f32[96,1024]{1,0:T(8,128)}, u32[]{:S(2)}) copy-start(f32[96,1024]{1,0:T(8,128)} %reduce-scatter.2.cloned.1.call-done) | copy-start | bytes 1179652
  273.2 8.1 %all-to-all-start = ((bf16[4,96,256]{2,1,0:T(8,128)(2,1)}), bf16[4,96,256]{2,1,0:T(8,128)(2,1)S(1)}, u32[]{:S(2)}, u32[]{:S(2)}) async-start(bf16[4,96,256]{2,1,0:T(8,128)(2,1)} %bitcast.79), calls=%async_computation.1 | async-start | bytes 393216 | tf_op jit(solution)/shard_map/all_to_all | solution.py:328
  292.2 9.8 %copy-start.5 = (bf16[3,1024,256]{2,1,0:T(8,128)(2,1)S(1)}, bf16[3,1024,256]{2,1,0:T(8,128)(2,1)}, u32[]{:S(2)}) copy-start(bf16[3,1024,256]{2,1,0:T(8,128)(2,1)} %param.23) | copy-start | bytes 4718596
Sparse Core Ops, SparseCore 0:
  21.1 131.0 all-gather.2
  155.2 68.5 all-gather.4
  226.3 22.7 reduce-scatter.1
